TPU v7x, 32 devices: a whole 2x2x4 slice. The times are simulated.
32 devices in a mesh: clips: 2 (over y), seq: 4 (over z), tp: 2 (over x), dp: 2 (over core).
Axes of the slice: x: 2, y: 2, z: 4, core: 2. Of those that a mesh axis runs over, the one named last changes fastest.
Arguments:
- video_query: bfloat16 [4, 512, 4096], P(('clips', 'dp'), 'seq', 'tp'), parts along dimension 0, may hold values from -384 to 384
- video_key: bfloat16 [4, 512, 4096], P(('clips', 'dp'), 'seq', 'tp'), parts along dimension 0, may hold values from -384 to 384
- video_value: bfloat16 [4, 512, 4096], P(('clips', 'dp'), 'seq', 'tp'), parts along dimension 0, may hold values from -6 to 6
- cross_query: bfloat16 [4, 512, 2048], P(('clips', 'dp'), 'seq', 'tp'), parts along dimension 0, may hold values from -384 to 384
- audio_key: bfloat16 [4, 32, 2048], P(('clips', 'dp'), 'seq', 'tp'), parts along dimension 0, may hold values from -384 to 384
- audio_value: bfloat16 [4, 32, 2048], P(('clips', 'dp'), 'seq', 'tp'), parts along dimension 0, may hold values from -6 to 6
- audio_query: bfloat16 [4, 32, 2048], P(('clips', 'dp'), 'seq', 'tp'), parts along dimension 0, may hold values from -384 to 384
- cross_key: bfloat16 [4, 512, 2048], P(('clips', 'dp'), 'seq', 'tp'), parts along dimension 0, may hold values from -384 to 384
- cross_value: bfloat16 [4, 512, 2048], P(('clips', 'dp'), 'seq', 'tp'), parts along dimension 0, may hold values from -6 to 6
- audio_input: bfloat16 [4, 32, 2048], P(('clips', 'dp'), 'seq'), parts along dimension 0, may hold values from -0.29882812 to 0.29882812
- norm_gain: float32 [2048], replicated, may hold values from 0.1 to 1.9
- up_weight: bfloat16 [2048, 8192], P('tp', 'seq'), may hold values from -0.125 to 0.125
- down_weight: bfloat16 [8192, 2048], P('seq', 'tp'), may hold values from -0.0625 to 0.0625
Outputs:
- video_mixed: bfloat16 [4, 512, 4096], P(('clips', 'dp'), 'seq', 'tp'), parts along dimension 0
- video_heard: bfloat16 [4, 512, 2048], P(('clips', 'dp'), 'seq', 'tp'), parts along dimension 0
- audio_seen: bfloat16 [4, 32, 2048], P(('clips', 'dp'), 'seq', 'tp'), parts along dimension 0
- audio_mlp: bfloat16 [4, 32, 2048], P(('clips', 'dp'), 'seq', 'tp'), parts along dimension 0
There are 2 independent parts, one for each index of `clips`. A program takes and returns all parts, laid end to end along the dimension named above; an argument that names none is the same for every part. Nothing has to cross between parts.
All inputs are finite; a program needn't handle non-finite values.
Results may differ from a plain program's by a relative error of at most 0.013.
Values may be sent and summed in bfloat16 or wider, within the bound.
A program may use at most 64 MiB of HBM per device.

v0:
```python
import math

import jax
import jax.numpy as jnp
from jax import lax
from jax.sharding import PartitionSpec as P

VHEAD = 128
CHEAD = 64


def attend_rows(queries, keys_in, values_in, head_count):
    head_size = queries.shape[1] // head_count
    query_heads = queries.reshape(queries.shape[0], head_count, head_size)
    key_heads = keys_in.reshape(keys_in.shape[0], head_count, head_size)
    value_heads = values_in.reshape(values_in.shape[0], head_count, head_size)
    scores = jnp.einsum(
        "qhd,khd->qhk", query_heads, key_heads, preferred_element_type=jnp.float32
    ) / math.sqrt(head_size)
    peak_value = jnp.max(scores, axis=2, keepdims=True)
    weights = jnp.exp(scores - peak_value)
    totals = jnp.sum(weights, axis=2)
    weighted = jnp.einsum(
        "qhk,khd->qhd",
        weights.astype(jnp.bfloat16),
        value_heads,
        preferred_element_type=jnp.float32,
    )
    result = weighted / totals[:, :, None]
    return result.reshape(queries.shape[0], head_count * head_size).astype(jnp.bfloat16)


def attend(queries, keys_in, values_in, head_count):
    row_total = queries.shape[0]
    block_rows = 512 if row_total % 512 == 0 else row_total
    pieces = queries.reshape(row_total // block_rows, block_rows, queries.shape[1])
    result = lax.map(
        lambda row_piece: attend_rows(row_piece, keys_in, values_in, head_count), pieces
    )
    return result.reshape(row_total, queries.shape[1])


def video_self(queries, keys_in, values_in):
    seq_count = lax.axis_size("seq")
    local_heads = queries.shape[1] // VHEAD
    dest_heads = max(local_heads // seq_count, 1)
    blocks = seq_count * dest_heads // local_heads
    groups = local_heads // dest_heads
    group_width = dest_heads * VHEAD
    token_count = queries.shape[0]
    block_tokens = token_count // blocks

    def spread(tensor):
        shaped = tensor.reshape(token_count, groups, group_width).transpose(1, 0, 2)
        shaped = jnp.broadcast_to(shaped[:, None], (groups, blocks, token_count, group_width))
        return shaped.reshape(seq_count, token_count, group_width)

    shaped = queries.reshape(blocks, block_tokens, groups, group_width).transpose(2, 0, 1, 3)
    own_queries = lax.all_to_all(
        shaped.reshape(seq_count, block_tokens, group_width),
        "seq",
        split_axis=0,
        concat_axis=0,
        tiled=True,
    )
    keys_all = lax.all_to_all(spread(keys_in), "seq", split_axis=0, concat_axis=0, tiled=True)
    values_all = lax.all_to_all(spread(values_in), "seq", split_axis=0, concat_axis=0, tiled=True)
    keys_all = keys_all.reshape(-1, group_width)
    values_all = values_all.reshape(-1, group_width)
    own_queries = own_queries.reshape(-1, group_width)
    attended = attend(own_queries, keys_all, values_all, dest_heads)
    returned = lax.all_to_all(
        attended.reshape(seq_count, block_tokens, group_width),
        "seq",
        split_axis=0,
        concat_axis=0,
        tiled=True,
    )
    returned = returned.reshape(groups, blocks, block_tokens, group_width).transpose(1, 2, 0, 3)
    return returned.reshape(token_count, groups * group_width)


def audio_listen(queries, keys_in, values_in, head_count):
    head_size = queries.shape[1] // head_count
    query_heads = queries.reshape(queries.shape[0], head_count, head_size)
    key_heads = keys_in.reshape(keys_in.shape[0], head_count, head_size)
    value_heads = values_in.reshape(values_in.shape[0], head_count, head_size)
    scores = jnp.einsum(
        "qhd,khd->qhk", query_heads, key_heads, preferred_element_type=jnp.float32
    ) / math.sqrt(head_size)
    local_peak = jnp.max(scores, axis=2)
    peak_value = lax.pmax(local_peak, "seq")
    weights = jnp.exp(scores - peak_value[:, :, None])
    totals = jnp.sum(weights, axis=2)
    weighted = jnp.einsum(
        "qhk,khd->qhd",
        weights.astype(jnp.bfloat16),
        value_heads,
        preferred_element_type=jnp.float32,
    )
    totals, weighted = (totals, weighted.reshape(queries.shape[0], head_count * head_size))
    totals, weighted = (
        lax.psum_scatter(totals, "seq", scatter_dimension=0, tiled=True),
        lax.psum_scatter(weighted, "seq", scatter_dimension=0, tiled=True),
    )
    return (weighted / jnp.repeat(totals, head_size, axis=1)).astype(jnp.bfloat16)


def audio_block(audio_rows, audio_seen, norm_gain, up_weight, down_weight):
    features = lax.all_gather(audio_seen, "tp", axis=1, tiled=True)
    residual = audio_rows.astype(jnp.float32) + features.astype(jnp.float32)
    scale_factor = lax.rsqrt(jnp.mean(residual * residual, axis=1, keepdims=True) + 1e-06)
    normed = (residual * scale_factor * norm_gain).astype(jnp.bfloat16)
    slice_width = up_weight.shape[0]
    own_features = lax.dynamic_slice_in_dim(
        normed, lax.axis_index("tp") * slice_width, slice_width, 1
    )
    partial_sum = jnp.dot(
        lax.all_gather(own_features, "seq", axis=0, tiled=True),
        up_weight,
        preferred_element_type=jnp.float32,
    )
    hidden = jax.nn.gelu(lax.psum(partial_sum, "tp")).astype(jnp.bfloat16)
    return lax.psum_scatter(
        jnp.dot(hidden, down_weight, preferred_element_type=jnp.float32),
        "seq",
        scatter_dimension=0,
        tiled=True,
    ).astype(jnp.bfloat16)


def body(
    video_query,
    video_key,
    video_value,
    cross_query,
    audio_key,
    audio_value,
    audio_query,
    cross_key,
    cross_value,
    audio_input,
    norm_gain,
    up_weight,
    down_weight,
):
    mixed_list, heard_list, seen_list, output_list = ([], [], [], [])
    cross_heads = cross_query.shape[2] // CHEAD
    mixed_list.append(video_self(video_query[0], video_key[0], video_value[0]))
    gathered_query = lax.all_gather(audio_query[0], "seq", axis=0, tiled=True)
    gathered_key = lax.all_gather(audio_key[0], "seq", axis=0, tiled=True)
    gathered_value = lax.all_gather(audio_value[0], "seq", axis=0, tiled=True)
    heard_list.append(attend(cross_query[0], gathered_key, gathered_value, cross_heads))
    audio_seen = audio_listen(gathered_query, cross_key[0], cross_value[0], cross_heads)
    seen_list.append(audio_seen)
    output_list.append(audio_block(audio_input[0], audio_seen, norm_gain, up_weight, down_weight))
    return (
        jnp.stack(mixed_list),
        jnp.stack(heard_list),
        jnp.stack(seen_list),
        jnp.stack(output_list),
    )


def solution(mesh):
    placed = (
        P(("clips", "dp"), "seq", "tp"),
        P(("clips", "dp"), "seq", "tp"),
        P(("clips", "dp"), "seq", "tp"),
        P(("clips", "dp"), "seq", "tp"),
        P(("clips", "dp"), "seq", "tp"),
        P(("clips", "dp"), "seq", "tp"),
        P(("clips", "dp"), "seq", "tp"),
        P(("clips", "dp"), "seq", "tp"),
        P(("clips", "dp"), "seq", "tp"),
        P(("clips", "dp"), "seq", None),
        P(),
        P("tp", "seq"),
        P("seq", "tp"),
    )
    return jax.shard_map(
        body,
        mesh=mesh,
        in_specs=placed,
        out_specs=(
            P(("clips", "dp"), "seq", "tp"),
            P(("clips", "dp"), "seq", "tp"),
            P(("clips", "dp"), "seq", "tp"),
            P(("clips", "dp"), "seq", "tp"),
        ),
        check_vma=False,
    )
```

profile of v0, /device:TPU:0, one launch (start us, length us, event | category | flops | bytes accessed | tf_op | source)
XLA Modules:
  0.0 171.0 jit_solution(16451558797304456168)
XLA Ops:
  7.2 2.0 %copy.100 = bf16[1,16,4,8,512]{4,3,1,2,0:T(8,128)(2,1)} copy(bf16[1,16,4,8,512]{4,3,2,1,0:T(8,128)(2,1)} %bitcast.77) | data formatting | bytes 1048576 | tf_op jit(solution)/shard_map/reshape;squeeze | solution.py:58
  9.2 6.3 %all-to-all-start.1 = ((bf16[4,128,512]{2,1,0:T(8,128)(2,1)}), bf16[4,128,512]{2,1,0:T(8,128)(2,1)S(1)}, u32[]{:S(2)}, u32[]{:S(2)}) async-start(bf16[4,128,512]{2,1,0:T(8,128)(2,1)} %bitcast.69), calls=%async_computation.1 | async-start | bytes 1048576 | tf_op jit(solution)/shard_map/all_to_all | solution.py:59
  15.5 1.2 copy.70
  16.7 1.1 copy.68
  17.9 17.8 %all-gather.2 = bf16[1,32,1024]{2,1,0:T(8,128)(2,1)S(1)} all-gather(bf16[1,8,1024]{2,1,0:T(8,128)(2,1)} %param.19), channel_id=4, replica_groups=mesh['clips'=2,'seq'=4,'tp'=2,'dp'=2] {'seq'}, dimensions={1}, use_global_device_ids=true | all-gather | bytes 81920 | tf_op jit(solution)/shard_map/all_gather | solution.py:150
  35.7 0.1 reshape.82
  35.8 0.3 fusion.57
  36.1 11.0 %pmax.7 = f32[32,16]{0,1:T(8,128)S(1)} all-reduce(f32[32,16]{0,1:T(8,128)S(1)} %get-tuple-element.56), channel_id=1, replica_groups=mesh['clips'=2,'seq'=4,'tp'=2,'dp'=2] {'seq'}, use_global_device_ids=true, to_apply=%region_5.6 | all-reduce | flops 512 | bytes 4096 | tf_op jit(solution)/shard_map/pmax | solution.py:92
  47.2 0.3 convolution_bitcast_fusion.1
  47.5 0.2 copy.71
  47.6 0.8 reshape.83
  48.5 0.4 reshape_squeeze.15
  48.9 0.9 copy.102
  49.7 0.4 reshape_squeeze.17
  50.1 0.9 copy.101
  51.0 0.2 copy.65
  51.2 13.2 %all-gather = bf16[1,32,1024]{2,1,0:T(8,128)(2,1)S(1)} all-gather(bf16[1,8,1024]{2,1,0:T(8,128)(2,1)S(1)} %copy-done.6), channel_id=2, replica_groups=mesh['clips'=2,'seq'=4,'tp'=2,'dp'=2] {'seq'}, dimensions={1}, use_global_device_ids=true | all-gather | bytes 81920 | tf_op jit(solution)/shard_map/all_gather | solution.py:151
  64.4 0.1 reshape.79
  64.5 0.3 fusion.34
  64.9 0.6 dynamic-slice
  66.1 15.7 %all-reduce = f32[32,16]{1,0:T(8,128)S(1)} all-reduce(f32[32,16]{1,0:T(8,128)S(1)} %copy.72), channel_id=6, replica_groups=mesh['clips'=2,'seq'=4,'tp'=2,'dp'=2] {'seq'}, use_global_device_ids=true, to_apply=%region_8.9.clone | all-reduce | flops 512 | bytes 4096
  82.0 0.2 fusion.56
  82.3 3.5 %all-to-all-start = ((bf16[4,128,512]{2,1,0:T(8,128)(2,1)}), bf16[4,128,512]{2,1,0:T(8,128)(2,1)S(1)}, u32[]{:S(2)}, u32[]{:S(2)}) async-start(bf16[4,128,512]{2,1,0:T(8,128)(2,1)} %bitcast.71), calls=%async_computation | async-start | bytes 1048576 | tf_op jit(solution)/shard_map/all_to_all | solution.py:66
  85.8 0.8 divide_convert_fusion
  86.6 4.4 %all_gather.18 = bf16[8,2048]{1,0:T(8,128)(2,1)S(1)} all-gather(bf16[8,1024]{1,0:T(8,128)(2,1)S(1)} %divide_convert_fusion), channel_id=1, replica_groups=mesh['clips'=2,'seq'=4,'tp'=2,'dp'=2] {'tp'}, dimensions={1}, use_global_device_ids=true | all-gather | bytes 49152 | tf_op jit(solution)/shard_map/all_gather | solution.py:110
  91.0 0.1 multiply_reduce_fusion
  91.2 13.9 %all_gather.19 = bf16[32,1024]{1,0:T(8,128)(2,1)S(1)} all-gather(bf16[8,1024]{1,0:T(8,128)(2,1)S(1)} %fusion.50), channel_id=1, replica_groups=mesh['clips'=2,'seq'=4,'tp'=2,'dp'=2] {'seq'}, dimensions={0}, use_global_device_ids=true | all-gather | bytes 81920 | tf_op jit(solution)/shard_map/all_gather | solution.py:119
  105.1 4.6 %all-to-all-start.2 = ((bf16[4,128,512]{2,1,0:T(8,128)(2,1)}), bf16[4,128,512]{2,1,0:T(8,128)(2,1)S(1)}, u32[]{:S(2)}, u32[]{:S(2)}) async-start(bf16[4,128,512]{2,1,0:T(8,128)(2,1)} %bitcast.70), calls=%async_computation.2 | async-start | bytes 1048576 | tf_op jit(solution)/shard_map/all_to_all | solution.py:67
  109.7 3.7 %fusion.58 = f32[32,2048]{1,0:T(8,128)} fusion(bf16[32,1024]{1,0:T(8,128)(2,1)S(1)} %all_gather.19, bf16[1024,2048]{1,0:T(8,128)(2,1)} %param.24), kind=kOutput, calls=%fused_computation.67 | convolution fusion | flops 134217728 | bytes 4521984 | tf_op jit(solution)/shard_map/dot_general | solution.py:118
  113.5 0.1 reshape.77
  113.7 0.7 bitcast_reduce_fusion
  114.5 1.9 %copy-done = f32[4,512,512]{2,1,0:T(8,128)} copy-done((f32[4,512,512]{2,1,0:T(8,128)}, f32[4,512,512]{2,1,0:T(8,128)S(1)}, u32[]{:S(2)}) %copy-start) | copy-done | bytes 4194328
  116.4 0.7 fusion.1
  117.1 7.5 %all-to-all-done.2 = bf16[4,128,512]{2,1,0:T(8,128)(2,1)S(1)} async-done(((bf16[4,128,512]{2,1,0:T(8,128)(2,1)}), bf16[4,128,512]{2,1,0:T(8,128)(2,1)S(1)}, u32[]{:S(2)}, u32[]{:S(2)}) %all-to-all-start.2) | async-done | bytes 524320 | tf_op jit(solution)/shard_map/all_to_all | solution.py:67
  124.8 3.4 %fusion.17 = bf16[512,4,128]{2,0,1:T(8,128)(2,1)S(1)} fusion(f32[4,512,512]{2,1,0:T(8,128)} %copy-done, f32[512,4]{0,1:T(4,128)S(1)} %get-tuple-element.52, bf16[512,4,128]{2,1,0:T(4,128)(2,1)S(1)} %reshape_reshape.11, f32[512,4]{0,1:T(4,128)S(1)} %fusion.1), kind=kOutput, calls=%fused_computation.18 | convolution fusion | flops 272105472 | bytes 5259264 | tf_op jit(solution)/shard_map/while/body/eval_jaxpr/qhk,khd->qhd/dot_general | solution.py:23
  128.2 0.4 copy.63
  128.6 1.0 convert_element_type.56
  129.6 3.5 %all-to-all-start.3 = ((bf16[4,128,512]{2,1,0:T(8,128)(2,1)}), bf16[4,128,512]{2,1,0:T(8,128)(2,1)S(1)}, u32[]{:S(2)}, u32[]{:S(2)}) async-start(bf16[4,128,512]{2,1,0:T(8,128)(2,1)} %convert_element_type.56), calls=%async_computation.3 | async-start | bytes 1048576 | tf_op jit(solution)/shard_map/all_to_all | solution.py:72
  133.1 5.3 %all-reduce.3.cloned.1.call-done = f32[32,2048]{1,0:T(8,128)} async-done(((f32[32,2048]{1,0:T(8,128)}), f32[32,2048]{1,0:T(8,128)}) %all-reduce.3.cloned.1.call-update) | async-done | bytes 262160 | tf_op jit(solution)/shard_map/psum | solution.py:123
  138.4 3.7 %fusion.38 = f32[32,1024]{1,0:T(8,128)} fusion(bf16[2048,1024]{1,0:T(8,128)(2,1)} %param.25, f32[32,2048]{1,0:T(8,128)} %all-reduce.3.cloned.1.call-done), kind=kOutput, calls=%fused_computation.41 | convolution fusion | flops 134807552 | bytes 4587520 | tf_op jit(solution)/shard_map/dot_general | solution.py:125
  142.1 13.3 %all-gather.1 = bf16[1,32,1024]{2,1,0:T(8,128)(2,1)S(1)} all-gather(bf16[1,8,1024]{2,1,0:T(8,128)(2,1)S(1)} %copy-done.7), channel_id=3, replica_groups=mesh['clips'=2,'seq'=4,'tp'=2,'dp'=2] {'seq'}, dimensions={1}, use_global_device_ids=true | all-gather | bytes 81920 | tf_op jit(solution)/shard_map/all_gather | solution.py:152
  155.4 0.1 reshape.81
  155.6 0.3 fusion.11
  155.8 0.9 copy.74
  156.7 5.1 %reduce-scatter.5.cloned.1.call-done = f32[8,1024]{1,0:T(8,128)} async-done(((f32[32,1024]{1,0:T(8,128)}), f32[8,1024]{1,0:T(8,128)}) %reduce-scatter.5.cloned.1.call-update) | async-done | bytes 32784 | tf_op jit(solution)/shard_map/reduce_scatter | solution.py:124
  161.8 1.4 convert_bitcast_fusion
  163.2 0.3 copy.64
  163.5 1.0 copy.73
  (39 shorter events, 0.9 us)
Async XLA Ops:
  7.2 41.3 %copy-start.1 = (bf16[1,128,2048]{2,1,0:T(8,128)(2,1)S(1)}, bf16[1,128,2048]{2,1,0:T(8,128)(2,1)}, u32[]{:S(2)}) copy-start(bf16[1,128,2048]{2,1,0:T(8,128)(2,1)} %param.14) | copy-start | bytes 1572868
  7.2 42.6 %copy-start.2 = (bf16[1,128,2048]{2,1,0:T(8,128)(2,1)S(1)}, bf16[1,128,2048]{2,1,0:T(8,128)(2,1)}, u32[]{:S(2)}) copy-start(bf16[1,128,2048]{2,1,0:T(8,128)(2,1)} %param.15) | copy-start | bytes 1572868
  9.2 73.1 %all-to-all-start.1 = ((bf16[4,128,512]{2,1,0:T(8,128)(2,1)}), bf16[4,128,512]{2,1,0:T(8,128)(2,1)S(1)}, u32[]{:S(2)}, u32[]{:S(2)}) async-start(bf16[4,128,512]{2,1,0:T(8,128)(2,1)} %bitcast.69), calls=%async_computation.1 | async-start | bytes 1048576 | tf_op jit(solution)/shard_map/all_to_all | solution.py:59
  15.5 35.5 %copy-start.3 = (bf16[1,128,1024]{2,1,0:T(8,128)(2,1)S(1)}, bf16[1,128,1024]{2,1,0:T(8,128)(2,1)}, u32[]{:S(2)}) copy-start(bf16[1,128,1024]{2,1,0:T(8,128)(2,1)} %param.16) | copy-start | bytes 786436
  15.5 35.7 %copy-start.6 = (bf16[1,8,1024]{2,1,0:T(8,128)(2,1)S(1)}, bf16[1,8,1024]{2,1,0:T(8,128)(2,1)}, u32[]{:S(2)}) copy-start(bf16[1,8,1024]{2,1,0:T(8,128)(2,1)} %param.17) | copy-start | bytes 49156
  15.5 70.3 %reduce-scatter.3.cloned.1.call-start = ((), (), s32[]{:S(2)}) async-start(), calls=%async_computation.6 | async-start | bytes 163840 | tf_op jit(solution)/shard_map/reduce_scatter | solution.py:104
  17.8 47.0 %copy-start.9 = (u32[32]{0:T(128)S(1)}, u32[32]{0:T(128)}, u32[]{:S(2)}) copy-start(u32[32]{0:T(128)} %constant.75) | copy-start | bytes 388
  17.8 64.2 %copy-start.8 = (f32[2048]{0:T(1024)S(1)}, f32[2048]{0:T(1024)}, u32[]{:S(2)}) copy-start(f32[2048]{0:T(1024)} %param.23) | copy-start | bytes 24580
  47.6 43.4 %copy-start.5 = (bf16[1,8,2048]{2,1,0:T(8,128)(2,1)S(1)}, bf16[1,8,2048]{2,1,0:T(8,128)(2,1)}, u32[]{:S(2)}) copy-start(bf16[1,8,2048]{2,1,0:T(8,128)(2,1)} %param.22) | copy-start | bytes 98308
  82.3 22.8 %all-to-all-start = ((bf16[4,128,512]{2,1,0:T(8,128)(2,1)}), bf16[4,128,512]{2,1,0:T(8,128)(2,1)S(1)}, u32[]{:S(2)}, u32[]{:S(2)}) async-start(bf16[4,128,512]{2,1,0:T(8,128)(2,1)} %bitcast.71), calls=%async_computation | async-start | bytes 1048576 | tf_op jit(solution)/shard_map/all_to_all | solution.py:66
  86.6 27.9 %copy-start.4 = (bf16[8,1024]{1,0:T(8,128)(2,1)}, bf16[8,1024]{1,0:T(8,128)(2,1)S(1)}, u32[]{:S(2)}) copy-start(bf16[8,1024]{1,0:T(8,128)(2,1)S(1)} %divide_convert_fusion) | copy-start | bytes 49156
  105.1 19.5 %all-to-all-start.2 = ((bf16[4,128,512]{2,1,0:T(8,128)(2,1)}), bf16[4,128,512]{2,1,0:T(8,128)(2,1)S(1)}, u32[]{:S(2)}, u32[]{:S(2)}) async-start(bf16[4,128,512]{2,1,0:T(8,128)(2,1)} %bitcast.70), calls=%async_computation.2 | async-start | bytes 1048576 | tf_op jit(solution)/shard_map/all_to_all | solution.py:67
  109.7 28.7 %all-reduce.3.cloned.1.call-start = ((), (), s32[]{:S(2)}) async-start(), calls=%async_computation.7 | async-start | bytes 524288 | tf_op jit(solution)/shard_map/psum | solution.py:123
  114.5 1.9 %copy-start = (f32[4,512,512]{2,1,0:T(8,128)}, f32[4,512,512]{2,1,0:T(8,128)S(1)}, u32[]{:S(2)}) copy-start(f32[4,512,512]{2,1,0:T(8,128)S(1)} %get-tuple-element.53) | copy-start | bytes 12582916
  128.1 14.0 %copy-start.7 = (bf16[1,8,1024]{2,1,0:T(8,128)(2,1)S(1)}, bf16[1,8,1024]{2,1,0:T(8,128)(2,1)}, u32[]{:S(2)}) copy-start(bf16[1,8,1024]{2,1,0:T(8,128)(2,1)} %param.18) | copy-start | bytes 49156
  129.6 33.6 %all-to-all-start.3 = ((bf16[4,128,512]{2,1,0:T(8,128)(2,1)}), bf16[4,128,512]{2,1,0:T(8,128)(2,1)S(1)}, u32[]{:S(2)}, u32[]{:S(2)}) async-start(bf16[4,128,512]{2,1,0:T(8,128)(2,1)} %convert_element_type.56), calls=%async_computation.3 | async-start | bytes 1048576 | tf_op jit(solution)/shard_map/all_to_all | solution.py:72
  133.0 28.8 %reduce-scatter.5.cloned.1.call-start = ((), (), s32[]{:S(2)}) async-start(), calls=%async_computation.8 | async-start | bytes 163840 | tf_op jit(solution)/shard_map/reduce_scatter | solution.py:124
Sparse Core Ops, SparseCore 0:
  48.6 17.6 reduce-scatter.2
  113.6 24.7 all-reduce.2
  142.2 19.5 reduce-scatter.4
where the time goes:
time: 172 us; the launch traced here: 171 us
  blocking collectives  89.4 us (52%)
  starting transfers between devices  18 us (10%)
  waiting for transfers between devices  18 us (10%)
  local copies, waits for them, and re-layouts  15 us (9%)
  between operations  14.7 us (9%)
  matrix products  12.6 us (7%)
  other arithmetic  3.38 us (2%)
    all_gather x1, blocking collectives, body(): gathered_query = lax.all_gather(audio_query[0], 'seq', axis=0, tiled=True)  17.8 us
    unnamed x1, blocking collectives  15.7 us
    all_gather x1, blocking collectives, audio_block(): lax.all_gather(own_features, 'seq', axis=0, tiled=True)  13.9 us
    all_gather x1, blocking collectives, body(): gathered_value = lax.all_gather(audio_value[0], 'seq', axis=0, tiled=True)  13.3 us
    all_gather x1, blocking collectives, body(): gathered_key = lax.all_gather(audio_key[0], 'seq', axis=0, tiled=True)  13.2 us
    pmax x1, blocking collectives, audio_listen(): peak_value = lax.pmax(local_peak, 'seq')  11 us
    all_to_all x1, waiting for transfers between devices, video_self(): lax.all_to_all(spread(values_in), 'seq', split_axis=0, concat_axis=0, til...  7.52 us
    unnamed x27, local copies, waits for them, and re-layouts  6.86 us
  transfers between devices with their start and end apart: 7, of which 3 were waited for; matrix products, arithmetic and copies ran while one was open for 15% of the time, Pallas kernels for 0%

commit v1 on v0

--- a/solution.py
+++ b/solution.py
@@ -1,12 +1,317 @@
+import functools
 import math
 
 import jax
 import jax.numpy as jnp
 from jax import lax
+from jax.experimental import pallas as pl
+from jax.experimental.pallas import tpu as pltpu
 from jax.sharding import PartitionSpec as P
 
 VHEAD = 128
 CHEAD = 64
+MESH = pl.DeviceIdType.MESH
+LOG2E = math.log2(math.e)
+CHUNKS = 4
+
+
+def dot_t(a, b):
+    return lax.dot_general(a, b, (((1,), (1,)), ((), ())), preferred_element_type=jnp.float32)
+
+
+def softmax_parts(q, k, scale):
+    s = dot_t(q, k)
+    peak = jnp.max(s, axis=1, keepdims=True)
+    p = jnp.exp2((s - peak) * (scale * LOG2E))
+    return p, peak * scale, jnp.sum(p, axis=1, keepdims=True)
+
+
+def pair_attend(q, k, v, scale):
+    low = lax.broadcasted_iota(jnp.int32, q.shape, 1) < CHEAD
+    zero = jnp.zeros_like(q)
+    both = jnp.concatenate([jnp.where(low, q, zero), jnp.where(low, zero, q)], axis=0)
+    p, peak, total = softmax_parts(both, k, scale)
+    o = jnp.dot(p.astype(jnp.bfloat16), v, preferred_element_type=jnp.float32)
+    return o, peak, total
+
+
+def fused_kernel(
+    n, tp,
+    vq, vk, vv, cq, ak, av, aq, ck, cv, ai, gain, up, down,
+    mixed, heard, seen, mlp,
+    qbuf, kbuf, vbuf, obuf, abuf, cqv, ckv, cvv, upv, downv, xsend, xrecv, ssbuf, nbuf, pbuf, rsend, rrecv,
+    v_send, v_recv, o_send, o_recv, a_send, a_recv, x_send, x_recv, s_send, s_recv,
+    n_send, n_recv, p_send, p_recv, r_send, r_recv, own_sem, oown_sem, load_sem,
+):
+    me = lax.axis_index("seq")
+    col = lax.axis_index("tp")
+    tokens = vq.shape[0]
+    hd = vq.shape[1] // VHEAD // n
+    rows, width = aq.shape
+    pairs = width // 128
+    units = up.shape[1]
+    step = units // CHUNKS
+    f32, bf16 = jnp.float32, jnp.bfloat16
+    peers = [lax.rem(me + d, n) for d in range(1, n)]
+    tp_peers = [lax.rem(col + d, tp) for d in range(1, tp)]
+
+    def remote(src, dst, ss, rs, where):
+        copy = pltpu.make_async_remote_copy(
+            src_ref=src, dst_ref=dst, send_sem=ss, recv_sem=rs, device_id=where, device_id_type=MESH
+        )
+        copy.start()
+        return copy
+
+    loads = []
+    for i, (src, dst) in enumerate(((ck, ckv), (cv, cvv), (cq, cqv), (up, upv), (down, downv))):
+        loads.append(pltpu.make_async_copy(src, dst, load_sem.at[i]))
+        loads[-1].start()
+    owns = []
+    for h in range(hd):
+        cols = pl.ds(pl.multiple_of((me * hd + h) * VHEAD, VHEAD), VHEAD)
+        owns.append([])
+        for i, (src, buf) in enumerate(((vq, qbuf), (vk, kbuf), (vv, vbuf))):
+            copy = pltpu.make_async_copy(src.at[:, cols], buf.at[h, me], own_sem.at[h, i])
+            copy.start()
+            owns[-1].append(copy)
+
+    barrier = pltpu.get_barrier_semaphore()
+    for p in peers:
+        pl.semaphore_signal(barrier, inc=1, device_id={"seq": p}, device_id_type=MESH)
+    for t in tp_peers:
+        pl.semaphore_signal(barrier, inc=1, device_id={"tp": t}, device_id_type=MESH)
+    pl.semaphore_wait(barrier, n - 1 + tp - 1)
+
+    sent = []
+
+    def send_video(h):
+        copies = []
+        for d, p in enumerate(peers):
+            cols = pl.ds(pl.multiple_of((p * hd + h) * VHEAD, VHEAD), VHEAD)
+            for i, (src, buf) in enumerate(((vq, qbuf), (vk, kbuf), (vv, vbuf))):
+                copies.append(
+                    remote(src.at[:, cols], buf.at[h, me], v_send.at[h, d, i], v_recv.at[h, d, i], {"seq": p})
+                )
+        sent.extend(copies)
+        return copies
+
+    def attend_video(h, copies):
+        for copy in owns[h]:
+            copy.wait()
+        for copy in copies:
+            copy.wait_recv()
+        k = kbuf[h].reshape(n * tokens, VHEAD)
+        v = vbuf[h].reshape(n * tokens, VHEAD)
+        cols = pl.ds(pl.multiple_of((me * hd + h) * VHEAD, VHEAD), VHEAD)
+        out = []
+        for d in range(1, n + 1):
+            p = lax.rem(me + d, n)
+            w, _, total = softmax_parts(qbuf[h, p], k, 1.0 / math.sqrt(VHEAD))
+            o = jnp.dot(w.astype(bf16), v, preferred_element_type=f32) / total
+            obuf[h, p] = o.astype(bf16)
+            if d < n:
+                out.append(
+                    remote(obuf.at[h, p], mixed.at[:, cols], o_send.at[h, d - 1], o_recv.at[h, d - 1], {"seq": p})
+                )
+        own = pltpu.make_async_copy(obuf.at[h, me], mixed.at[:, cols], oown_sem.at[h])
+        own.start()
+        return out, own
+
+    gathers = []
+    for i, src in enumerate((aq, ak, av)):
+        for d, p in enumerate(peers):
+            gathers.append(remote(src, abuf.at[i, me], a_send.at[i, d], a_recv.at[i, d], {"seq": p}))
+        abuf[i, me] = src[...]
+    sent.extend(gathers)
+    video = [send_video(0)]
+
+    for copy in loads[:2]:
+        copy.wait()
+    for copy in gathers:
+        copy.wait_recv()
+
+    def whole(i):
+        return jnp.concatenate([abuf[i, s].astype(f32) for s in range(n)], axis=0).astype(bf16)
+
+    scale = 1.0 / math.sqrt(CHEAD)
+    total_rows = n * rows
+    q_all = whole(0)
+    lane = lax.broadcasted_iota(jnp.int32, (total_rows, 128), 1)
+    peaks = jnp.zeros((total_rows, 128), f32)
+    totals = jnp.ones((total_rows, 128), f32)
+    for j in range(pairs):
+        at = slice(j * 128, (j + 1) * 128)
+        o, peak, total = pair_attend(q_all[:, at], ckv[:, at], cvv[:, at], scale)
+        picked = jnp.where(lane < CHEAD, o[:total_rows], o[total_rows:])
+        xsend[:, :, at] = picked.reshape(n, rows, 128)
+        for half in range(2):
+            part = slice(half * total_rows, (half + 1) * total_rows)
+            peaks = jnp.where(lane == 2 * j + half, peak[part], peaks)
+            totals = jnp.where(lane == 2 * j + half, total[part], totals)
+    xsend[:, :, width : width + 128] = peaks.reshape(n, rows, 128)
+    xsend[:, :, width + 128 : width + 256] = totals.reshape(n, rows, 128)
+    exchanges = []
+    for d, p in enumerate(peers):
+        exchanges.append(remote(xsend.at[p], xrecv.at[me], x_send.at[d], x_recv.at[d], {"seq": p}))
+    sent.extend(exchanges)
+    xrecv[me] = xsend[me]
+    for h in range(1, min(2, hd)):
+        video.append(send_video(h))
+
+    loads[2].wait()
+    k_all, v_all = whole(1), whole(2)
+    wide = lax.broadcasted_iota(jnp.int32, (tokens, 128), 1)
+    for j in range(pairs):
+        at = slice(j * 128, (j + 1) * 128)
+        o, _, total = pair_attend(cqv[:, at], k_all[:, at], v_all[:, at], scale)
+        o = o / total
+        heard[:, at] = jnp.where(wide < CHEAD, o[:tokens], o[tokens:]).astype(bf16)
+
+    for copy in exchanges:
+        copy.wait_recv()
+    peak = xrecv[0, :, width : width + 128]
+    for s in range(1, n):
+        peak = jnp.maximum(peak, xrecv[s, :, width : width + 128])
+    factors = [jnp.exp(xrecv[s, :, width : width + 128] - peak) for s in range(n)]
+    total = sum(factors[s] * xrecv[s, :, width + 128 : width + 256] for s in range(n))
+    factors = [f / total for f in factors]
+    low = lax.broadcasted_iota(jnp.int32, (rows, 128), 1) < CHEAD
+    pieces = []
+    for j in range(pairs):
+        at = slice(j * 128, (j + 1) * 128)
+        value = jnp.zeros((rows, 128), f32)
+        for s in range(n):
+            f = factors[s]
+            value += jnp.where(low, f[:, 2 * j : 2 * j + 1], f[:, 2 * j + 1 : 2 * j + 2]) * xrecv[s, :, at]
+        pieces.append(value)
+    seen_bf = jnp.concatenate(pieces, axis=1).astype(bf16)
+    seen[...] = seen_bf
+
+    mine = pl.ds(pl.multiple_of(col * width, 128), width)
+    residual = ai[:, mine].astype(f32) + seen_bf.astype(f32)
+    square = jnp.sum(residual * residual, axis=1, keepdims=True)
+    ssbuf[col] = jnp.broadcast_to(square, (rows, 128))
+    squares = []
+    for d, t in enumerate(tp_peers):
+        squares.append(remote(ssbuf.at[col], ssbuf.at[col], s_send.at[d], s_recv.at[d], {"tp": t}))
+    sent.extend(squares)
+    for copy in squares:
+        copy.wait_recv()
+    square = sum(ssbuf[t] for t in range(tp))[:, 0:1]
+    factor = lax.rsqrt(square / (width * tp) + 1e-6)
+    nbuf[me] = (residual * factor * gain[:, mine]).astype(bf16)
+    normed = []
+    for d, p in enumerate(peers):
+        normed.append(remote(nbuf.at[me], nbuf.at[me], n_send.at[d], n_recv.at[d], {"seq": p}))
+    sent.extend(normed)
+    for h in range(2, min(3, hd)):
+        video.append(send_video(h))
+
+    outs = [attend_video(0, video[0])]
+
+    loads[3].wait()
+    for copy in normed:
+        copy.wait_recv()
+    x = jnp.concatenate([nbuf[s].astype(f32) for s in range(n)], axis=0).astype(bf16)
+    partials = []
+    for c in range(CHUNKS):
+        pbuf[col, c] = jnp.dot(x, upv[:, c * step : (c + 1) * step], preferred_element_type=f32)
+        for d, t in enumerate(tp_peers):
+            partials.append(
+                remote(pbuf.at[col, c], pbuf.at[col, c], p_send.at[c, d], p_recv.at[c, d], {"tp": t})
+            )
+    sent.extend(partials)
+    for h in range(3, hd):
+        video.append(send_video(h))
+
+    if hd > 1:
+        outs.append(attend_video(1, video[1]))
+
+    loads[4].wait()
+    for copy in partials:
+        copy.wait_recv()
+    acc = jnp.zeros((total_rows, width), f32)
+    for c in range(CHUNKS):
+        hidden = jax.nn.gelu(sum(pbuf[t, c] for t in range(tp)), approximate=True).astype(bf16)
+        acc += jnp.dot(hidden, downv[c * step : (c + 1) * step, :], preferred_element_type=f32)
+    rsend[...] = acc.reshape(n, rows, width)
+    results = []
+    for d, p in enumerate(peers):
+        results.append(remote(rsend.at[p], rrecv.at[me], r_send.at[d], r_recv.at[d], {"seq": p}))
+    sent.extend(results)
+    rrecv[me] = rsend[me]
+
+    for h in range(2, hd):
+        outs.append(attend_video(h, video[h]))
+
+    for copy in results:
+        copy.wait_recv()
+    mlp[...] = sum(rrecv[s] for s in range(n)).astype(bf16)
+
+    for out, own in outs:
+        for copy in out:
+            copy.wait()
+        own.wait()
+    for copy in sent:
+        copy.wait_send()
+
+
+def fused(n, tp, args):
+    vq, vk, vv, cq, ak, av, aq, ck, cv, ai, gain, up, down = args
+    tokens, vwidth = vq.shape
+    hd = vwidth // VHEAD // n
+    rows, width = aq.shape
+    units = up.shape[1]
+    bf16, f32 = jnp.bfloat16, jnp.float32
+    anywhere = pl.BlockSpec(memory_space=pl.ANY)
+    vmem = pl.BlockSpec(memory_space=pltpu.VMEM)
+    dma = pltpu.SemaphoreType.DMA
+    head = pltpu.VMEM((hd, n, tokens, VHEAD), bf16)
+    cross = pltpu.VMEM((tokens, width), bf16)
+    z, t = max(n - 1, 1), max(tp - 1, 1)
+    return pl.pallas_call(
+        functools.partial(fused_kernel, n, tp),
+        out_shape=(
+            jax.ShapeDtypeStruct((tokens, vwidth), bf16),
+            jax.ShapeDtypeStruct((tokens, width), bf16),
+            jax.ShapeDtypeStruct((rows, width), bf16),
+            jax.ShapeDtypeStruct((rows, width), bf16),
+        ),
+        in_specs=[anywhere] * 4 + [vmem] * 3 + [anywhere] * 2 + [vmem] * 2 + [anywhere] * 2,
+        out_specs=(anywhere, vmem, vmem, vmem),
+        scratch_shapes=[
+            head, head, head, head,
+            pltpu.VMEM((3, n, rows, width), bf16),
+            cross, cross, cross,
+            pltpu.VMEM(up.shape, bf16),
+            pltpu.VMEM(down.shape, bf16),
+            pltpu.VMEM((n, rows, width + 256), f32),
+            pltpu.VMEM((n, rows, width + 256), f32),
+            pltpu.VMEM((tp, rows, 128), f32),
+            pltpu.VMEM((n, rows, width), bf16),
+            pltpu.VMEM((tp, CHUNKS, n * rows, units // CHUNKS), f32),
+            pltpu.VMEM((n, rows, width), f32),
+            pltpu.VMEM((n, rows, width), f32),
+            dma((hd, z, 3)), dma((hd, z, 3)), dma((hd, z)), dma((hd, z)),
+            dma((3, z)), dma((3, z)), dma((z,)), dma((z,)), dma((t,)), dma((t,)),
+            dma((z,)), dma((z,)), dma((CHUNKS, t)), dma((CHUNKS, t)), dma((z,)), dma((z,)),
+            dma((hd, 3)), dma((hd,)), dma((5,)),
+        ],
+        compiler_params=pltpu.CompilerParams(collective_id=0, has_side_effects=True),
+    )(vq, vk, vv, cq, ak, av, aq, ck, cv, ai, gain.reshape(1, -1), up, down)
+
+
+def fits(n, vq, aq, up):
+    heads = vq.shape[2] // VHEAD
+    return (
+        heads % n == 0
+        and vq.shape[1] % 16 == 0
+        and aq.shape[1] % 8 == 0
+        and aq.shape[2] % 128 == 0
+        and aq.shape[2] // CHEAD <= 128
+        and up.shape[0] == aq.shape[2]
+        and up.shape[1] % (128 * CHUNKS) == 0
+    )
 
 
 def attend_rows(queries, keys_in, values_in, head_count):
@@ -144,6 +449,12 @@
     up_weight,
     down_weight,
 ):
+    if fits(lax.axis_size("seq"), video_query, audio_query, up_weight):
+        args = (video_query, video_key, video_value, cross_query, audio_key, audio_value)
+        args += (audio_query, cross_key, cross_value, audio_input)
+        args = tuple(a[0] for a in args) + (norm_gain, up_weight, down_weight)
+        outs = fused(lax.axis_size("seq"), lax.axis_size("tp"), args)
+        return tuple(out[None] for out in outs)
     mixed_list, heard_list, seen_list, output_list = ([], [], [], [])
     cross_heads = cross_query.shape[2] // CHEAD
     mixed_list.append(video_self(video_query[0], video_key[0], video_value[0]))

time: 172 us -> 72.8 us (0.42)
  blocking collectives: 89.4 us -> 0 us
  Pallas kernels: 0 us -> 65.5 us
  starting transfers between devices: 18 us -> 0 us
  waiting for transfers between devices: 18 us -> 0 us
  between operations: 14.7 us -> 0.65 us
  matrix products: 12.6 us -> 0 us
  local copies, waits for them, and re-layouts: 15 us -> 6.2 us
  other arithmetic: 3.38 us -> 0 us
    pallas_call x0 -> x1, Pallas kernels: none -> 65.5 us  [fused(): pl.pallas_call(functools.partial(fused_kernel, n, tp), out_shape=(jax.Sha...]
    all_gather x5 -> x0, blocking collectives: 62.6 us -> none  [the longest x1 17.8 us: body(): gathered_query = lax.all_gather(audio_query[0], 'seq', axis=0, tiled=True)]
    all_to_all x4 -> x0, starting transfers between devices: 17.9 us -> none  [the longest x1 6.35 us: video_self(): lax.all_to_all(shaped.reshape(seq_count, block_tokens, group_width), 'seq...]
    unnamed x1 -> x0, blocking collectives: 15.7 us -> none
    dot_general x8 -> x0, matrix products: 12.6 us -> none  [the longest x1 3.72 us: audio_block(): jnp.dot(lax.all_gather(own_features, 'seq', axis=0, tiled=True), up_weigh...]
    pmax x1 -> x0, blocking collectives: 11 us -> none  [audio_listen(): peak_value = lax.pmax(local_peak, 'seq')]
    all_to_all x4 -> x0, waiting for transfers between devices: 7.53 us -> none  [the longest x1 7.52 us: video_self(): lax.all_to_all(spread(values_in), 'seq', split_axis=0, concat_axis=0, til...]
    psum x1 -> x0, waiting for transfers between devices: 5.27 us -> none  [audio_block(): hidden = jax.nn.gelu(lax.psum(partial_sum, 'tp')).astype(jnp.bfloat16)]
  transfers between devices with their start and end apart: 7 -> 0, of which waited for: 3 -> 0; matrix products, arithmetic and copies ran while one was open for 15% -> 0% of each run, Pallas kernels for 0% -> 0%
where the time goes in v1:
time: 72.8 us; the launch traced here: 72.3 us
  Pallas kernels  65.5 us (90%)
  local copies, waits for them, and re-layouts  6.2 us (9%)
    pallas_call x1, Pallas kernels, fused(): pl.pallas_call(functools.partial(fused_kernel, n, tp), out_shape=(jax.Sha...  65.5 us
    unnamed x4, local copies, waits for them, and re-layouts  6.2 us

profile of v1, /device:TPU:0, one launch (start us, length us, event | category | flops | bytes accessed | tf_op | source)
XLA Modules:
  0.0 72.3 jit_solution(7056162587950796396)
XLA Ops:
  0.6 65.5 %shard_map.156 = (bf16[128,2048]{1,0:T(8,128)(2,1)}, bf16[128,1024]{1,0:T(8,128)(2,1)}, bf16[8,1024]{1,0:T(8,128)(2,1)}, bf16[8,1024]{1,0:T(8,128)(2,1)}) custom-call(bf16[128,2048]{1,0:T(8,128)(2,1)} %bitcast.15, bf16[128,2048]{1,0:T(8,128)(2,1)} %bitcast.16, bf16[128,2048]{1,0:T(8,128)(2,1)} %bitcast.17, bf16[128,1024]{1,0:T(8,128)(2,1)} %bitcast.19, ...), custom_call_target="tpu_custom_call" | custom-call | tf_op jit(solution)/shard_map/pallas_call | solution.py:272
  66.1 1.9 %copy.21 = bf16[1,128,2048]{2,1,0:T(8,128)(2,1)} copy(bf16[1,128,2048]{2,1,0:T(8,128)(2,1)} %bitcast.18) | data formatting | bytes 1048576
  68.0 1.7 %copy.22 = bf16[1,128,1024]{2,1,0:T(8,128)(2,1)} copy(bf16[1,128,1024]{2,1,0:T(8,128)(2,1)} %bitcast.22) | data formatting | bytes 524288
  69.7 1.3 %copy.23 = bf16[1,8,1024]{2,1,0:T(8,128)(2,1)} copy(bf16[1,8,1024]{2,1,0:T(8,128)(2,1)} %bitcast.28) | data formatting | bytes 32768
  71.0 1.3 %copy.24 = bf16[1,8,1024]{2,1,0:T(8,128)(2,1)} copy(bf16[1,8,1024]{2,1,0:T(8,128)(2,1)} %bitcast.27) | data formatting | bytes 32768

commit v2 on v1

--- a/solution.py
+++ b/solution.py
@@ -35,12 +35,26 @@
     return o, peak, total
 
 
+def partners(me, n):
+    if n & (n - 1):
+        return [lax.rem(me + d, n) for d in range(1, n)]
+    found = []
+    for flip in range(n - 1, 0, -1):
+        place, bit = me * 0, 1
+        while bit < n:
+            digit = lax.rem(lax.div(me, bit), 2)
+            place = place + bit * ((1 - digit) if flip & bit else digit)
+            bit *= 2
+        found.append(place)
+    return found
+
+
 def fused_kernel(
     n, tp,
     vq, vk, vv, cq, ak, av, aq, ck, cv, ai, gain, up, down,
     mixed, heard, seen, mlp,
-    qbuf, kbuf, vbuf, obuf, abuf, cqv, ckv, cvv, upv, downv, xsend, xrecv, ssbuf, nbuf, pbuf, rsend, rrecv,
-    v_send, v_recv, o_send, o_recv, a_send, a_recv, x_send, x_recv, s_send, s_recv,
+    qbuf, kbuf, vbuf, obuf, abuf, cqv, ckv, cvv, upv, downv, xsend, xrecv, tsend, trecv, hbuf, sbuf, mbuf, ssbuf, nbuf, pbuf, rsend, rrecv,
+    v_send, v_recv, o_send, o_recv, a_send, a_recv, x_send, x_recv, t_send, t_recv, s_send, s_recv,
     n_send, n_recv, p_send, p_recv, r_send, r_recv, own_sem, oown_sem, load_sem,
 ):
     me = lax.axis_index("seq")
@@ -52,7 +66,7 @@
     units = up.shape[1]
     step = units // CHUNKS
     f32, bf16 = jnp.float32, jnp.bfloat16
-    peers = [lax.rem(me + d, n) for d in range(1, n)]
+    peers = partners(me, n)
     tp_peers = [lax.rem(col + d, tp) for d in range(1, tp)]
 
     def remote(src, dst, ss, rs, where):
@@ -104,25 +118,25 @@
         v = vbuf[h].reshape(n * tokens, VHEAD)
         cols = pl.ds(pl.multiple_of((me * hd + h) * VHEAD, VHEAD), VHEAD)
         out = []
-        for d in range(1, n + 1):
-            p = lax.rem(me + d, n)
+        for d, p in enumerate(peers + [me]):
             w, _, total = softmax_parts(qbuf[h, p], k, 1.0 / math.sqrt(VHEAD))
             o = jnp.dot(w.astype(bf16), v, preferred_element_type=f32) / total
             obuf[h, p] = o.astype(bf16)
-            if d < n:
-                out.append(
-                    remote(obuf.at[h, p], mixed.at[:, cols], o_send.at[h, d - 1], o_recv.at[h, d - 1], {"seq": p})
-                )
+            if d < n - 1:
+                out.append(remote(obuf.at[h, p], mixed.at[:, cols], o_send.at[h, d], o_recv.at[h, d], {"seq": p}))
         own = pltpu.make_async_copy(obuf.at[h, me], mixed.at[:, cols], oown_sem.at[h])
         own.start()
         return out, own
 
-    gathers = []
+    relay = n == 4
+    gathers, direct = [], []
     for i, src in enumerate((aq, ak, av)):
         for d, p in enumerate(peers):
-            gathers.append(remote(src, abuf.at[i, me], a_send.at[i, d], a_recv.at[i, d], {"seq": p}))
+            if i == 0 or not relay or d > 0:
+                copy = remote(src, abuf.at[i, me], a_send.at[i, d], a_recv.at[i, d], {"seq": p})
+                (direct if i else gathers).append(copy)
         abuf[i, me] = src[...]
-    sent.extend(gathers)
+    sent.extend(gathers + direct)
     video = [send_video(0)]
 
     for copy in loads[:2]:
@@ -137,43 +151,55 @@
     total_rows = n * rows
     q_all = whole(0)
     lane = lax.broadcasted_iota(jnp.int32, (total_rows, 128), 1)
-    peaks = jnp.zeros((total_rows, 128), f32)
-    totals = jnp.ones((total_rows, 128), f32)
+    stats = jnp.ones((total_rows, 128), f32)
     for j in range(pairs):
         at = slice(j * 128, (j + 1) * 128)
         o, peak, total = pair_attend(q_all[:, at], ckv[:, at], cvv[:, at], scale)
         picked = jnp.where(lane < CHEAD, o[:total_rows], o[total_rows:])
-        xsend[:, :, at] = picked.reshape(n, rows, 128)
+        xsend[:, :, at] = picked.reshape(n, rows, 128).astype(bf16)
         for half in range(2):
             part = slice(half * total_rows, (half + 1) * total_rows)
-            peaks = jnp.where(lane == 2 * j + half, peak[part], peaks)
-            totals = jnp.where(lane == 2 * j + half, total[part], totals)
-    xsend[:, :, width : width + 128] = peaks.reshape(n, rows, 128)
-    xsend[:, :, width + 128 : width + 256] = totals.reshape(n, rows, 128)
+            stats = jnp.where(lane == 2 * j + half, peak[part], stats)
+            stats = jnp.where(lane == 64 + 2 * j + half, total[part], stats)
+    tsend[...] = stats.reshape(n, rows, 128)
     exchanges = []
     for d, p in enumerate(peers):
+        exchanges.append(remote(tsend.at[p], trecv.at[me], t_send.at[d], t_recv.at[d], {"seq": p}))
         exchanges.append(remote(xsend.at[p], xrecv.at[me], x_send.at[d], x_recv.at[d], {"seq": p}))
     sent.extend(exchanges)
     xrecv[me] = xsend[me]
+    trecv[me] = tsend[me]
     for h in range(1, min(2, hd)):
         video.append(send_video(h))
 
     loads[2].wait()
+    for copy in direct:
+        copy.wait_recv()
+    if relay:
+        passed = []
+        for i in (1, 2):
+            slot = abuf.at[i, peers[1]]
+            passed.append(remote(slot, slot, a_send.at[i, 0], a_recv.at[i, 0], {"seq": peers[2]}))
+        sent.extend(passed)
+        for copy in passed:
+            copy.wait_recv()
     k_all, v_all = whole(1), whole(2)
     wide = lax.broadcasted_iota(jnp.int32, (tokens, 128), 1)
     for j in range(pairs):
         at = slice(j * 128, (j + 1) * 128)
         o, _, total = pair_attend(cqv[:, at], k_all[:, at], v_all[:, at], scale)
         o = o / total
-        heard[:, at] = jnp.where(wide < CHEAD, o[:tokens], o[tokens:]).astype(bf16)
+        hbuf[:, at] = jnp.where(wide < CHEAD, o[:tokens], o[tokens:]).astype(bf16)
+    results_out = [pltpu.make_async_copy(hbuf, heard, load_sem.at[5])]
+    results_out[-1].start()
 
     for copy in exchanges:
         copy.wait_recv()
-    peak = xrecv[0, :, width : width + 128]
+    peak = trecv[0]
     for s in range(1, n):
-        peak = jnp.maximum(peak, xrecv[s, :, width : width + 128])
-    factors = [jnp.exp(xrecv[s, :, width : width + 128] - peak) for s in range(n)]
-    total = sum(factors[s] * xrecv[s, :, width + 128 : width + 256] for s in range(n))
+        peak = jnp.maximum(peak, trecv[s])
+    factors = [jnp.exp(trecv[s] - peak) for s in range(n)]
+    total = sum(factors[s] * pltpu.roll(trecv[s], 64, 1) for s in range(n))
     factors = [f / total for f in factors]
     low = lax.broadcasted_iota(jnp.int32, (rows, 128), 1) < CHEAD
     pieces = []
@@ -182,10 +208,12 @@
         value = jnp.zeros((rows, 128), f32)
         for s in range(n):
             f = factors[s]
-            value += jnp.where(low, f[:, 2 * j : 2 * j + 1], f[:, 2 * j + 1 : 2 * j + 2]) * xrecv[s, :, at]
+            value += jnp.where(low, f[:, 2 * j : 2 * j + 1], f[:, 2 * j + 1 : 2 * j + 2]) * xrecv[s, :, at].astype(f32)
         pieces.append(value)
     seen_bf = jnp.concatenate(pieces, axis=1).astype(bf16)
-    seen[...] = seen_bf
+    sbuf[...] = seen_bf
+    results_out.append(pltpu.make_async_copy(sbuf, seen, load_sem.at[6]))
+    results_out[-1].start()
 
     mine = pl.ds(pl.multiple_of(col * width, 128), width)
     residual = ai[:, mine].astype(f32) + seen_bf.astype(f32)
@@ -234,7 +262,7 @@
     for c in range(CHUNKS):
         hidden = jax.nn.gelu(sum(pbuf[t, c] for t in range(tp)), approximate=True).astype(bf16)
         acc += jnp.dot(hidden, downv[c * step : (c + 1) * step, :], preferred_element_type=f32)
-    rsend[...] = acc.reshape(n, rows, width)
+    rsend[...] = acc.reshape(n, rows, width).astype(bf16)
     results = []
     for d, p in enumerate(peers):
         results.append(remote(rsend.at[p], rrecv.at[me], r_send.at[d], r_recv.at[d], {"seq": p}))
@@ -246,12 +274,16 @@
 
     for copy in results:
         copy.wait_recv()
-    mlp[...] = sum(rrecv[s] for s in range(n)).astype(bf16)
+    mbuf[...] = sum(rrecv[s].astype(f32) for s in range(n)).astype(bf16)
+    results_out.append(pltpu.make_async_copy(mbuf, mlp, load_sem.at[7]))
+    results_out[-1].start()
 
     for out, own in outs:
         for copy in out:
             copy.wait()
         own.wait()
+    for copy in results_out:
+        copy.wait()
     for copy in sent:
         copy.wait_send()
 
@@ -278,27 +310,59 @@
             jax.ShapeDtypeStruct((rows, width), bf16),
         ),
         in_specs=[anywhere] * 4 + [vmem] * 3 + [anywhere] * 2 + [vmem] * 2 + [anywhere] * 2,
-        out_specs=(anywhere, vmem, vmem, vmem),
+        out_specs=(anywhere,) * 4,
         scratch_shapes=[
             head, head, head, head,
             pltpu.VMEM((3, n, rows, width), bf16),
             cross, cross, cross,
             pltpu.VMEM(up.shape, bf16),
             pltpu.VMEM(down.shape, bf16),
-            pltpu.VMEM((n, rows, width + 256), f32),
-            pltpu.VMEM((n, rows, width + 256), f32),
+            pltpu.VMEM((n, rows, width), bf16),
+            pltpu.VMEM((n, rows, width), bf16),
+            pltpu.VMEM((n, rows, 128), f32),
+            pltpu.VMEM((n, rows, 128), f32),
+            cross,
+            pltpu.VMEM((rows, width), bf16),
+            pltpu.VMEM((rows, width), bf16),
             pltpu.VMEM((tp, rows, 128), f32),
             pltpu.VMEM((n, rows, width), bf16),
             pltpu.VMEM((tp, CHUNKS, n * rows, units // CHUNKS), f32),
-            pltpu.VMEM((n, rows, width), f32),
-            pltpu.VMEM((n, rows, width), f32),
+            pltpu.VMEM((n, rows, width), bf16),
+            pltpu.VMEM((n, rows, width), bf16),
             dma((hd, z, 3)), dma((hd, z, 3)), dma((hd, z)), dma((hd, z)),
-            dma((3, z)), dma((3, z)), dma((z,)), dma((z,)), dma((t,)), dma((t,)),
+            dma((3, z)), dma((3, z)), dma((z,)), dma((z,)), dma((z,)), dma((z,)), dma((t,)), dma((t,)),
             dma((z,)), dma((z,)), dma((CHUNKS, t)), dma((CHUNKS, t)), dma((z,)), dma((z,)),
-            dma((hd, 3)), dma((hd,)), dma((5,)),
+            dma((hd, 3)), dma((hd,)), dma((8,)),
         ],
         compiler_params=pltpu.CompilerParams(collective_id=0, has_side_effects=True),
     )(vq, vk, vv, cq, ak, av, aq, ck, cv, ai, gain.reshape(1, -1), up, down)
+
+
+def hand_over(*refs):
+    count = (len(refs) - 2) // 3
+    sources, targets, buffers = refs[:count], refs[count : 2 * count], refs[2 * count : 3 * count]
+    into, out = refs[3 * count :]
+    coming = [pltpu.make_async_copy(s, b, into.at[i]) for i, (s, b) in enumerate(zip(sources, buffers))]
+    going = [pltpu.make_async_copy(b, t, out.at[i]) for i, (b, t) in enumerate(zip(buffers, targets))]
+    for copy in coming:
+        copy.start()
+    for first, second in zip(coming, going):
+        first.wait()
+        second.start()
+    for copy in going:
+        copy.wait()
+
+
+def deliver(arrays):
+    anywhere = pl.BlockSpec(memory_space=pl.ANY)
+    return pl.pallas_call(
+        hand_over,
+        out_shape=tuple(jax.ShapeDtypeStruct(a.shape, a.dtype) for a in arrays),
+        in_specs=[anywhere] * len(arrays),
+        out_specs=(anywhere,) * len(arrays),
+        scratch_shapes=[pltpu.VMEM(a.shape, a.dtype) for a in arrays]
+        + [pltpu.SemaphoreType.DMA((len(arrays),))] * 2,
+    )(*arrays)
 
 
 def fits(n, vq, aq, up):
@@ -308,7 +372,7 @@
         and vq.shape[1] % 16 == 0
         and aq.shape[1] % 8 == 0
         and aq.shape[2] % 128 == 0
-        and aq.shape[2] // CHEAD <= 128
+        and aq.shape[2] // CHEAD <= 64
         and up.shape[0] == aq.shape[2]
         and up.shape[1] % (128 * CHUNKS) == 0
     )
@@ -453,7 +517,7 @@
         args = (video_query, video_key, video_value, cross_query, audio_key, audio_value)
         args += (audio_query, cross_key, cross_value, audio_input)
         args = tuple(a[0] for a in args) + (norm_gain, up_weight, down_weight)
-        outs = fused(lax.axis_size("seq"), lax.axis_size("tp"), args)
+        outs = deliver(fused(lax.axis_size("seq"), lax.axis_size("tp"), args))
         return tuple(out[None] for out in outs)
     mixed_list, heard_list, seen_list, output_list = ([], [], [], [])
     cross_heads = cross_query.shape[2] // CHEAD

time: 72.8 us -> 63.8 us (0.88)
  local copies, waits for them, and re-layouts: 6.2 us -> 0 us
  Pallas kernels: 65.5 us -> 62.9 us
    unnamed x4 -> x0, local copies, waits for them, and re-layouts: 6.2 us -> none
    pallas_call x1, Pallas kernels: 65.5 us -> 60.9 us  [fused(): pl.pallas_call(functools.partial(fused_kernel, n, tp), out_shape=(jax.Sha...]
    pallas_call x0 -> x1, Pallas kernels: none -> 1.99 us  [deliver(): pl.pallas_call(hand_over, out_shape=tuple((jax.ShapeDtypeStruct(a.shape,...]
where the time goes in v2:
time: 63.8 us; the launch traced here: 63.6 us
  Pallas kernels  62.9 us (99%)
  between operations  0.64 us (1%)
    pallas_call x1, Pallas kernels, fused(): pl.pallas_call(functools.partial(fused_kernel, n, tp), out_shape=(jax.Sha...  60.9 us
    pallas_call x1, Pallas kernels, deliver(): pl.pallas_call(hand_over, out_shape=tuple((jax.ShapeDtypeStruct(a.shape,...  1.99 us

profile of v2, /device:TPU:0, one launch (start us, length us, event | category | flops | bytes accessed | tf_op | source)
XLA Modules:
  0.0 63.6 jit_solution(10013009263268680034)
XLA Ops:
  0.6 60.9 %shard_map.156 = (bf16[128,2048]{1,0:T(8,128)(2,1)}, bf16[128,1024]{1,0:T(8,128)(2,1)}, bf16[8,1024]{1,0:T(8,128)(2,1)}, bf16[8,1024]{1,0:T(8,128)(2,1)}) custom-call(bf16[128,2048]{1,0:T(8,128)(2,1)} %bitcast.15, bf16[128,2048]{1,0:T(8,128)(2,1)} %bitcast.16, bf16[128,2048]{1,0:T(8,128)(2,1)} %bitcast.17, bf16[128,1024]{1,0:T(8,128)(2,1)} %bitcast.18, ...), custom_call_target="tpu_custom_call" | custom-call | tf_op jit(solution)/shard_map/pallas_call | solution.py:304
  61.6 2.0 %shard_map.157 = (bf16[128,2048]{1,0:T(8,128)(2,1)}, bf16[128,1024]{1,0:T(8,128)(2,1)}, bf16[8,1024]{1,0:T(8,128)(2,1)}, bf16[8,1024]{1,0:T(8,128)(2,1)}) custom-call(bf16[128,2048]{1,0:T(8,128)(2,1)} %get-tuple-element.12.refs_0_, bf16[128,1024]{1,0:T(8,128)(2,1)} %get-tuple-element.13.refs_1_, bf16[8,1024]{1,0:T(8,128)(2,1)} %get-tuple-element.14.refs_2_, ...), custom_call_target="tpu_custom_call" | custom-call | tf_op jit(solution)/shard_map/pallas_call | solution.py:358

commit v3 on v2

--- a/solution.py
+++ b/solution.py
@@ -53,7 +53,7 @@
     n, tp,
     vq, vk, vv, cq, ak, av, aq, ck, cv, ai, gain, up, down,
     mixed, heard, seen, mlp,
-    qbuf, kbuf, vbuf, obuf, abuf, cqv, ckv, cvv, upv, downv, xsend, xrecv, tsend, trecv, hbuf, sbuf, mbuf, ssbuf, nbuf, pbuf, rsend, rrecv,
+    qbuf, kbuf, vbuf, obuf, abuf, cqv, ckv, cvv, upv, downv, aiv, gainv, xsend, xrecv, tsend, trecv, hbuf, sbuf, mbuf, ssbuf, nbuf, pbuf, rsend, rrecv,
     v_send, v_recv, o_send, o_recv, a_send, a_recv, x_send, x_recv, t_send, t_recv, s_send, s_recv,
     n_send, n_recv, p_send, p_recv, r_send, r_recv, own_sem, oown_sem, load_sem,
 ):
@@ -76,8 +76,16 @@
         copy.start()
         return copy
 
+    barrier = pltpu.get_barrier_semaphore()
+    for p in peers:
+        pl.semaphore_signal(barrier, inc=1, device_id={"seq": p}, device_id_type=MESH)
+    for t in tp_peers:
+        pl.semaphore_signal(barrier, inc=1, device_id={"tp": t}, device_id_type=MESH)
+
     loads = []
-    for i, (src, dst) in enumerate(((ck, ckv), (cv, cvv), (cq, cqv), (up, upv), (down, downv))):
+    stays = ((ck, ckv), (cv, cvv), (cq, cqv), (up, upv), (down, downv), (ai, aiv), (gain, gainv))
+    stays += tuple((src, abuf.at[i, me]) for i, src in enumerate((aq, ak, av)))
+    for i, (src, dst) in enumerate(stays):
         loads.append(pltpu.make_async_copy(src, dst, load_sem.at[i]))
         loads[-1].start()
     owns = []
@@ -89,11 +97,6 @@
             copy.start()
             owns[-1].append(copy)
 
-    barrier = pltpu.get_barrier_semaphore()
-    for p in peers:
-        pl.semaphore_signal(barrier, inc=1, device_id={"seq": p}, device_id_type=MESH)
-    for t in tp_peers:
-        pl.semaphore_signal(barrier, inc=1, device_id={"tp": t}, device_id_type=MESH)
     pl.semaphore_wait(barrier, n - 1 + tp - 1)
 
     sent = []
@@ -135,11 +138,10 @@
             if i == 0 or not relay or d > 0:
                 copy = remote(src, abuf.at[i, me], a_send.at[i, d], a_recv.at[i, d], {"seq": p})
                 (direct if i else gathers).append(copy)
-        abuf[i, me] = src[...]
     sent.extend(gathers + direct)
     video = [send_video(0)]
 
-    for copy in loads[:2]:
+    for copy in loads[:2] + loads[5:]:
         copy.wait()
     for copy in gathers:
         copy.wait_recv()
@@ -190,7 +192,7 @@
         o, _, total = pair_attend(cqv[:, at], k_all[:, at], v_all[:, at], scale)
         o = o / total
         hbuf[:, at] = jnp.where(wide < CHEAD, o[:tokens], o[tokens:]).astype(bf16)
-    results_out = [pltpu.make_async_copy(hbuf, heard, load_sem.at[5])]
+    results_out = [pltpu.make_async_copy(hbuf, heard, load_sem.at[10])]
     results_out[-1].start()
 
     for copy in exchanges:
@@ -212,11 +214,11 @@
         pieces.append(value)
     seen_bf = jnp.concatenate(pieces, axis=1).astype(bf16)
     sbuf[...] = seen_bf
-    results_out.append(pltpu.make_async_copy(sbuf, seen, load_sem.at[6]))
+    results_out.append(pltpu.make_async_copy(sbuf, seen, load_sem.at[11]))
     results_out[-1].start()
 
     mine = pl.ds(pl.multiple_of(col * width, 128), width)
-    residual = ai[:, mine].astype(f32) + seen_bf.astype(f32)
+    residual = aiv[:, mine].astype(f32) + seen_bf.astype(f32)
     square = jnp.sum(residual * residual, axis=1, keepdims=True)
     ssbuf[col] = jnp.broadcast_to(square, (rows, 128))
     squares = []
@@ -227,7 +229,7 @@
         copy.wait_recv()
     square = sum(ssbuf[t] for t in range(tp))[:, 0:1]
     factor = lax.rsqrt(square / (width * tp) + 1e-6)
-    nbuf[me] = (residual * factor * gain[:, mine]).astype(bf16)
+    nbuf[me] = (residual * factor * gainv[:, mine]).astype(bf16)
     normed = []
     for d, p in enumerate(peers):
         normed.append(remote(nbuf.at[me], nbuf.at[me], n_send.at[d], n_recv.at[d], {"seq": p}))
@@ -275,7 +277,7 @@
     for copy in results:
         copy.wait_recv()
     mbuf[...] = sum(rrecv[s].astype(f32) for s in range(n)).astype(bf16)
-    results_out.append(pltpu.make_async_copy(mbuf, mlp, load_sem.at[7]))
+    results_out.append(pltpu.make_async_copy(mbuf, mlp, load_sem.at[12]))
     results_out[-1].start()
 
     for out, own in outs:
@@ -296,7 +298,6 @@
     units = up.shape[1]
     bf16, f32 = jnp.bfloat16, jnp.float32
     anywhere = pl.BlockSpec(memory_space=pl.ANY)
-    vmem = pl.BlockSpec(memory_space=pltpu.VMEM)
     dma = pltpu.SemaphoreType.DMA
     head = pltpu.VMEM((hd, n, tokens, VHEAD), bf16)
     cross = pltpu.VMEM((tokens, width), bf16)
@@ -304,19 +305,21 @@
     return pl.pallas_call(
         functools.partial(fused_kernel, n, tp),
         out_shape=(
-            jax.ShapeDtypeStruct((tokens, vwidth), bf16),
-            jax.ShapeDtypeStruct((tokens, width), bf16),
-            jax.ShapeDtypeStruct((rows, width), bf16),
-            jax.ShapeDtypeStruct((rows, width), bf16),
+            pltpu.VMEM((tokens, vwidth), bf16),
+            pltpu.VMEM((tokens, width), bf16),
+            pltpu.VMEM((rows, width), bf16),
+            pltpu.VMEM((rows, width), bf16),
         ),
-        in_specs=[anywhere] * 4 + [vmem] * 3 + [anywhere] * 2 + [vmem] * 2 + [anywhere] * 2,
-        out_specs=(anywhere,) * 4,
+        in_specs=[anywhere] * 13,
+        out_specs=(pl.BlockSpec(memory_space=pltpu.VMEM),) * 4,
         scratch_shapes=[
             head, head, head, head,
             pltpu.VMEM((3, n, rows, width), bf16),
             cross, cross, cross,
             pltpu.VMEM(up.shape, bf16),
             pltpu.VMEM(down.shape, bf16),
+            pltpu.VMEM(ai.shape, bf16),
+            pltpu.VMEM((1, gain.shape[0]), f32),
             pltpu.VMEM((n, rows, width), bf16),
             pltpu.VMEM((n, rows, width), bf16),
             pltpu.VMEM((n, rows, 128), f32),
@@ -332,36 +335,29 @@
             dma((hd, z, 3)), dma((hd, z, 3)), dma((hd, z)), dma((hd, z)),
             dma((3, z)), dma((3, z)), dma((z,)), dma((z,)), dma((z,)), dma((z,)), dma((t,)), dma((t,)),
             dma((z,)), dma((z,)), dma((CHUNKS, t)), dma((CHUNKS, t)), dma((z,)), dma((z,)),
-            dma((hd, 3)), dma((hd,)), dma((8,)),
+            dma((hd, 3)), dma((hd,)), dma((13,)),
         ],
         compiler_params=pltpu.CompilerParams(collective_id=0, has_side_effects=True),
     )(vq, vk, vv, cq, ak, av, aq, ck, cv, ai, gain.reshape(1, -1), up, down)
 
 
 def hand_over(*refs):
-    count = (len(refs) - 2) // 3
-    sources, targets, buffers = refs[:count], refs[count : 2 * count], refs[2 * count : 3 * count]
-    into, out = refs[3 * count :]
-    coming = [pltpu.make_async_copy(s, b, into.at[i]) for i, (s, b) in enumerate(zip(sources, buffers))]
-    going = [pltpu.make_async_copy(b, t, out.at[i]) for i, (b, t) in enumerate(zip(buffers, targets))]
-    for copy in coming:
+    count = (len(refs) - 1) // 2
+    copies = [pltpu.make_async_copy(refs[i], refs[count + i], refs[-1].at[i]) for i in range(count)]
+    for copy in copies:
         copy.start()
-    for first, second in zip(coming, going):
-        first.wait()
-        second.start()
-    for copy in going:
+    for copy in copies:
         copy.wait()
 
 
 def deliver(arrays):
-    anywhere = pl.BlockSpec(memory_space=pl.ANY)
+    arrays = [pltpu.with_memory_space_constraint(a, pltpu.VMEM) for a in arrays]
     return pl.pallas_call(
         hand_over,
         out_shape=tuple(jax.ShapeDtypeStruct(a.shape, a.dtype) for a in arrays),
-        in_specs=[anywhere] * len(arrays),
-        out_specs=(anywhere,) * len(arrays),
-        scratch_shapes=[pltpu.VMEM(a.shape, a.dtype) for a in arrays]
-        + [pltpu.SemaphoreType.DMA((len(arrays),))] * 2,
+        in_specs=[pl.BlockSpec(memory_space=pltpu.VMEM)] * len(arrays),
+        out_specs=(pl.BlockSpec(memory_space=pl.ANY),) * len(arrays),
+        scratch_shapes=[pltpu.SemaphoreType.DMA((len(arrays),))],
     )(*arrays)
 
 

time: 63.8 us -> 62 us (0.972)
  Pallas kernels: 62.9 us -> 61.2 us
    pallas_call x1, Pallas kernels: 1.99 us -> 0.92 us  [deliver(): pl.pallas_call(hand_over, out_shape=tuple((jax.ShapeDtypeStruct(a.shape,...]
where the time goes in v3:
time: 62 us; the launch traced here: 61.9 us
  Pallas kernels  61.2 us (99%)
  between operations  0.64 us (1%)
    pallas_call x1, Pallas kernels, fused(): pl.pallas_call(functools.partial(fused_kernel, n, tp), out_shape=(pltpu.V...  60.3 us

profile of v3, /device:TPU:0, one launch (start us, length us, event | category | flops | bytes accessed | tf_op | source)
XLA Modules:
  0.0 61.9 jit_solution(10796575222479947566)
XLA Ops:
  0.6 60.3 %shard_map.156 = (bf16[128,2048]{1,0:T(8,128)(2,1)S(1)}, bf16[128,1024]{1,0:T(8,128)(2,1)S(1)}, bf16[8,1024]{1,0:T(8,128)(2,1)S(1)}, bf16[8,1024]{1,0:T(8,128)(2,1)S(1)}) custom-call(bf16[128,2048]{1,0:T(8,128)(2,1)} %bitcast.15, bf16[128,2048]{1,0:T(8,128)(2,1)} %bitcast.16, bf16[128,2048]{1,0:T(8,128)(2,1)} %bitcast.17, bf16[128,1024]{1,0:T(8,128)(2,1)} %bitcast.18, ...), custom_call_target="tpu_custom_call" | custom-call | tf_op jit(solution)/shard_map/pallas_call | solution.py:305
  61.0 0.9 %shard_map.157 = (bf16[128,2048]{1,0:T(8,128)(2,1)}, bf16[128,1024]{1,0:T(8,128)(2,1)}, bf16[8,1024]{1,0:T(8,128)(2,1)}, bf16[8,1024]{1,0:T(8,128)(2,1)}) custom-call(bf16[128,2048]{1,0:T(8,128)(2,1)S(1)} %get-tuple-element.12.refs_0_, bf16[128,1024]{1,0:T(8,128)(2,1)S(1)} %get-tuple-element.13.refs_1_, bf16[8,1024]{1,0:T(8,128)(2,1)S(1)} %get-tuple-element.14.refs_2_, ...), custom_call_target="tpu_custom_call" | custom-call | tf_op jit(solution)/shard_map/pallas_call | solution.py:355

commit v4 on v3

--- a/solution.py
+++ b/solution.py
@@ -232,16 +232,24 @@
     nbuf[me] = (residual * factor * gainv[:, mine]).astype(bf16)
     normed = []
     for d, p in enumerate(peers):
-        normed.append(remote(nbuf.at[me], nbuf.at[me], n_send.at[d], n_recv.at[d], {"seq": p}))
+        if not relay or d > 0:
+            normed.append(remote(nbuf.at[me], nbuf.at[me], n_send.at[d], n_recv.at[d], {"seq": p}))
     sent.extend(normed)
     for h in range(2, min(3, hd)):
         video.append(send_video(h))
 
-    outs = [attend_video(0, video[0])]
-
     loads[3].wait()
     for copy in normed:
         copy.wait_recv()
+    if relay:
+        slot = nbuf.at[peers[1]]
+        passed = remote(slot, slot, n_send.at[0], n_recv.at[0], {"seq": peers[2]})
+        sent.append(passed)
+
+    outs = [attend_video(0, video[0])]
+
+    if relay:
+        passed.wait_recv()
     x = jnp.concatenate([nbuf[s].astype(f32) for s in range(n)], axis=0).astype(bf16)
     partials = []
     for c in range(CHUNKS):

time: 62 us -> 61.3 us (0.989)
  Pallas kernels: 61.2 us -> 60.5 us
    pallas_call x1, Pallas kernels: 60.3 us -> 59.6 us  [fused(): pl.pallas_call(functools.partial(fused_kernel, n, tp), out_shape=(pltpu.V...]
where the time goes in v4:
time: 61.3 us; the launch traced here: 61.2 us
  Pallas kernels  60.5 us (99%)
  between operations  0.64 us (1%)
    pallas_call x1, Pallas kernels, fused(): pl.pallas_call(functools.partial(fused_kernel, n, tp), out_shape=(pltpu.V...  59.6 us

profile of v4, /device:TPU:0, one launch (start us, length us, event | category | flops | bytes accessed | tf_op | source)
XLA Modules:
  0.0 61.2 jit_solution(5767939867744791770)
XLA Ops:
  0.6 59.6 %shard_map.156 = (bf16[128,2048]{1,0:T(8,128)(2,1)S(1)}, bf16[128,1024]{1,0:T(8,128)(2,1)S(1)}, bf16[8,1024]{1,0:T(8,128)(2,1)S(1)}, bf16[8,1024]{1,0:T(8,128)(2,1)S(1)}) custom-call(bf16[128,2048]{1,0:T(8,128)(2,1)} %bitcast.15, bf16[128,2048]{1,0:T(8,128)(2,1)} %bitcast.16, bf16[128,2048]{1,0:T(8,128)(2,1)} %bitcast.17, bf16[128,1024]{1,0:T(8,128)(2,1)} %bitcast.18, ...), custom_call_target="tpu_custom_call" | custom-call | tf_op jit(solution)/shard_map/pallas_call | solution.py:313
  60.3 0.9 %shard_map.157 = (bf16[128,2048]{1,0:T(8,128)(2,1)}, bf16[128,1024]{1,0:T(8,128)(2,1)}, bf16[8,1024]{1,0:T(8,128)(2,1)}, bf16[8,1024]{1,0:T(8,128)(2,1)}) custom-call(bf16[128,2048]{1,0:T(8,128)(2,1)S(1)} %get-tuple-element.12.refs_0_, bf16[128,1024]{1,0:T(8,128)(2,1)S(1)} %get-tuple-element.13.refs_1_, bf16[8,1024]{1,0:T(8,128)(2,1)S(1)} %get-tuple-element.14.refs_2_, ...), custom_call_target="tpu_custom_call" | custom-call | tf_op jit(solution)/shard_map/pallas_call | solution.py:363
